TPU v7x, 32 devices: a whole 2x2x4 slice. The times are simulated.
32 devices in a mesh: lon: 4 (over x, core), frame: 8 (over z, y).
Axes of the slice: x: 2, y: 2, z: 4, core: 2. Of those that a mesh axis runs over, the one named last changes fastest.
Arguments:
- layer_input: bfloat16 [8, 16, 512, 128], P('frame', None, 'lon'), may hold values from -6 to 6
- hidden_saved: bfloat16 [8, 16, 512, 128], P('frame', None, 'lon'), as said below
- conv_weight: bfloat16 [3, 3, 128, 128], replicated, may hold values from -0.1875 to 0.1875
- queries: bfloat16 [2048, 128], P('lon'), may hold values from -6 to 6
- corr_cotangent: bfloat16 [8, 49, 2048], P('frame', None, 'lon'), may hold values from -0.59765625 to 0.59765625
- window_rows: int32 [8, 2048], P('frame', 'lon'), may hold values from 0 to 9
- window_cols: int32 [8, 2048], P('frame', 'lon'), may hold values from -3 to 124
- owner_strip: int32 [8, 2048, 1], P('frame', 'lon'), may hold values from 0 to 3; in each aligned block of 512 rows (0 to 511, 512 to 1023, ..., all dimensions but the last counted through in order) at most 128 rows name the same one
Outputs:
- query_grad: float32 [2048, 128], P(('lon', 'frame'))
- first_weight_grad: float32 [3, 3, 128, 128], replicated
- second_weight_grad: float32 [3, 3, 128, 128], replicated
Inputs may be any that keep to these rules, and one draw needn't show every extreme that they name: `hidden_saved`: rectifier outputs: zero or positive, a third or more of them exactly zero. `owner_strip`: in each frame, at most 128 of the 512 tracks homed on one strip name the same owning strip.
All inputs are finite; a program needn't handle non-finite values.
Results may differ from a plain program's by a relative error of at most 0.0045.
Values may be sent and summed in bfloat16 or wider, within the bound.
A program may use at most 64 MiB of HBM per device.

v0:
```python
import functools
import math

import jax
import jax.numpy as jnp
from jax import lax
from jax.experimental import pallas as pl
from jax.experimental.pallas import tpu as pltpu
from jax.sharding import PartitionSpec as P

WIN = 7
WIDE = 144
EXT = 160
BF = jnp.bfloat16
F32 = jnp.float32
MESH = pl.DeviceIdType.MESH


def dot(a, b):
    return jnp.dot(a, b, preferred_element_type=F32)


def kernel(
    dims,
    x_ref, h_ref, w_ref, q_ref, cot_ref, rows_ref, cols_ref, own_ref,
    query_out, first_out, second_out,
    hext, xext, gext, xh, xx, xg, feat, wb, fgrad, gt, spread,
    cm, pt, qall, cmall,
    pay_send, pay_recv, halo_send, halo_recv, edge_send, edge_recv,
    ret_send, ret_recv, retall, qg_send, qg_own, qg_recv,
    grads, w1_send, w1_recv, acc, w2_own, w2_send, w2_recv, ag1, ag2, wide_out,
    pay_s, pay_r, halo_s, halo_r, edge_s, edge_r, ret_s, ret_r, qg_s, qg_r,
    w1_s, w1_r, w2_s, w2_r, a1_s, a1_r, a2_s, a2_r,
):
    lon_n, frame_n, rows_n, cols_n, chans, tracks, cap, chunk, scale = dims
    lon, frame = lax.axis_index("lon"), lax.axis_index("frame")
    slots = lon_n * cap
    half = rows_n // 2

    def lon_id(steps):
        return lax.rem(lon + steps + lon_n, lon_n)

    def frame_id(steps):
        return lax.rem(frame + steps + frame_n, frame_n)

    def remote(src, dst, send, recv, where):
        return pltpu.make_async_remote_copy(
            src_ref=src, dst_ref=dst, send_sem=send, recv_sem=recv,
            device_id=where, device_id_type=MESH,
        )

    barrier = pltpu.get_barrier_semaphore()
    for step in range(1, lon_n):
        pl.semaphore_signal(barrier, inc=1, device_id={"lon": lon_id(step)}, device_id_type=MESH)
    for step in range(1, frame_n):
        pl.semaphore_signal(barrier, inc=1, device_id={"frame": frame_id(step)}, device_id_type=MESH)

    halo_send[...] = jnp.zeros_like(halo_send)
    halo_send[0, :, 0:4] = h_ref[:, cols_n - 8 :].astype(F32)[:, 4:8].astype(BF)
    halo_send[0, :, 4:5] = x_ref[:, cols_n - 8 :].astype(F32)[:, 7:8].astype(BF)
    halo_send[1, :, 0:4] = h_ref[:, 0:8].astype(F32)[:, 0:4].astype(BF)
    halo_send[1, :, 4:5] = x_ref[:, 0:8].astype(F32)[:, 0:1].astype(BF)

    owners = own_ref[...]
    marks = (owners == lax.broadcasted_iota(jnp.int32, (16, tracks), 0)).astype(F32)
    earlier = (
        lax.broadcasted_iota(jnp.int32, (tracks, tracks), 0)
        < lax.broadcasted_iota(jnp.int32, (tracks, tracks), 1)
    ).astype(F32).astype(BF)
    before = dot(marks.astype(BF), earlier)
    rank = jnp.sum(before * marks, axis=0, keepdims=True).astype(jnp.int32)
    slot = owners * cap + rank
    cm[...] = jnp.zeros_like(cm)
    for i in range(WIN):
        cm[8 * i : 8 * i + WIN, :] = cot_ref[WIN * i : WIN * i + WIN, :].astype(F32)
    cm[56:57, :] = rows_ref[...].astype(F32)
    cm[57:58, :] = (cols_ref[...] + 3).astype(F32)
    cm_half = cm[...].astype(BF)

    pl.semaphore_wait(barrier, lon_n - 1 + frame_n - 1)
    halos = [
        remote(halo_send.at[0], halo_recv.at[0], halo_s.at[0], halo_r.at[0], {"lon": lon_id(1)}),
        remote(halo_send.at[1], halo_recv.at[1], halo_s.at[1], halo_r.at[1], {"lon": lon_id(-1)}),
    ]
    for copy in halos:
        copy.start()
    pays = []
    for step in list(range(1, lon_n)) + [0]:
        local = slot - lon_id(step) * cap
        hot = (local == lax.broadcasted_iota(jnp.int32, (cap, tracks), 0)).astype(F32).astype(BF)
        pt[step * cap : (step + 1) * cap, :] = hot
        q_part = dot(hot, q_ref[...]).astype(BF)
        c_part = lax.dot_general(
            cm_half, hot, (((1,), (1,)), ((), ())), preferred_element_type=F32
        )
        if step:
            pay_send[step - 1, 0:cap, :] = q_part
            pay_send[step - 1, cap : cap + 64, :] = c_part.astype(BF)
            copy = remote(
                pay_send.at[step - 1], pay_recv.at[step - 1], pay_s.at[step - 1],
                pay_r.at[step - 1], {"lon": lon_id(step)},
            )
            copy.start()
            pays.append(copy)
        else:
            qall[0:cap, :] = q_part
            cmall[:, 0:cap] = c_part

    for a in range(3):
        for b in range(3):
            tap = w_ref[2 - a, (2 - b) * chans : (3 - b) * chans, :].astype(F32)
            wb[a, b * chans : (b + 1) * chans, :] = tap.T.astype(BF)

    def fill(ext, src):
        ext[...] = jnp.zeros_like(ext)

        @pl.loop(0, rows_n)
        def _(r):
            ext[r + 1, 16 : 16 + cols_n, :] = src[r].astype(F32)

    def side_by_side(ext, out):
        @pl.loop(0, rows_n + 2)
        def _(r):
            for b in range(3):
                out[r, :, b * chans : (b + 1) * chans] = ext[r, 7 + b : 7 + b + WIDE, :].astype(BF)

    fill(hext, h_ref)
    fill(xext, x_ref)
    for copy in halos:
        copy.wait()
    prior = halo_recv[0].astype(F32)
    later = halo_recv[1].astype(F32)
    hext[1 : rows_n + 1, 12:16, :] = prior[:, 0:4]
    hext[1 : rows_n + 1, 16 + cols_n : 20 + cols_n, :] = later[:, 0:4]
    xext[1 : rows_n + 1, 15:16, :] = prior[:, 4:5]
    xext[1 : rows_n + 1, 16 + cols_n : 17 + cols_n, :] = later[:, 4:5]
    side_by_side(hext, xh)

    def conv(source, weight, r0):
        total = None
        for a in range(3):
            block = source[r0 + a : r0 + a + half].reshape(half * WIDE, 3 * chans)
            term = dot(block, weight[a])
            total = term if total is None else total + term
        return total

    for g in range(2):
        feat[g * half * WIDE : (g + 1) * half * WIDE, :] = conv(xh, w_ref, g * half).astype(BF)
    side_by_side(xext, xx)

    def spread_block(step):
        lanes = slice(step * cap, (step + 1) * cap)
        rows_t = cmall[56:57, lanes].astype(jnp.int32)
        cols_t = cmall[57:58, lanes].astype(jnp.int32) + 5
        placed = []
        for r in range(rows_n):
            value = jnp.zeros((8, cap), F32)
            for i in range(WIN):
                if 0 <= r - i <= rows_n - WIN:
                    value = jnp.where(rows_t == r - i, cmall[8 * i : 8 * i + 8, lanes], value)
            placed.append(value)

        @pl.loop(0, WIDE // 16)
        def _(tile):
            offset = lax.broadcasted_iota(jnp.int32, (16, cap), 0) + tile * 16 - cols_t
            hits = [offset == j for j in range(WIN)]
            for r in range(rows_n):
                value = jnp.zeros((16, cap), F32)
                for j in range(WIN):
                    value = jnp.where(hits[j], placed[r][j : j + 1, :], value)
                start = pl.multiple_of(r * WIDE + tile * 16, 16)
                spread[pl.ds(start, 16), lanes] = value.astype(BF)

    spread_block(0)
    for step in range(1, lon_n):
        pays[step - 1].wait()
        qall[step * cap : (step + 1) * cap, :] = pay_recv[step - 1, 0:cap, :]
        cmall[:, step * cap : (step + 1) * cap] = pay_recv[step - 1, cap : cap + 64, :].astype(F32)
        spread_block(step)

    for g in range(2):
        cells = slice(g * half * WIDE, (g + 1) * half * WIDE)
        fgrad[g * half : (g + 1) * half] = dot(spread[cells, :], qall[...]).reshape(
            half, WIDE, chans
        )
    edge_send[0, :, 0:4] = fgrad[:, 7 + cols_n : 11 + cols_n, :]
    edge_send[1, :, 0:4] = fgrad[:, 5:9, :]
    edge_send[:, :, 4:8] = jnp.zeros((2, rows_n, 4, chans), F32)
    edges = [
        remote(edge_send.at[0], edge_recv.at[0], edge_s.at[0], edge_r.at[0], {"lon": lon_id(1)}),
        remote(edge_send.at[1], edge_recv.at[1], edge_s.at[1], edge_r.at[1], {"lon": lon_id(-1)}),
    ]
    for copy in edges:
        copy.start()

    slot_grads = lax.dot_general(
        feat[...], spread[...], (((0,), (0,)), ((), ())), preferred_element_type=F32
    )
    retall[:, 0:cap] = slot_grads[:, 0:cap].astype(BF)
    returns = []
    for step in range(1, lon_n):
        ret_send[step - 1] = slot_grads[:, step * cap : (step + 1) * cap].astype(BF)
        copy = remote(
            ret_send.at[step - 1], ret_recv.at[step - 1], ret_s.at[step - 1],
            ret_r.at[step - 1], {"lon": lon_id(-step)},
        )
        copy.start()
        returns.append(copy)

    gext[...] = jnp.zeros_like(gext)
    for copy in edges:
        copy.wait()
    gext[1 : rows_n + 1, 16 : 16 + cols_n, :] = fgrad[:, 8 : 8 + cols_n, :]
    gext[1 : rows_n + 1, 15:19, :] = fgrad[:, 7:11, :] + edge_recv[0, :, 0:4]
    gext[1 : rows_n + 1, 13 + cols_n : 17 + cols_n, :] = (
        fgrad[:, 5 + cols_n : 9 + cols_n, :] + edge_recv[1, :, 0:4]
    )
    side_by_side(gext, xg)

    column = lax.broadcasted_iota(jnp.int32, (half, WIDE, chans), 1)
    inside = (column >= 8) & (column < 8 + cols_n)

    def weight_terms(which, source):
        for a in range(3):
            block = source[a : a + rows_n].reshape(rows_n * WIDE, 3 * chans)
            term = dot(gt[...], block) * scale
            for b in range(3):
                tap = term[:, b * chans : (b + 1) * chans].T
                grads[which, 3 * a + b] = tap
                for d in range(lon_n):
                    part = tap[d * (chans // lon_n) : (d + 1) * (chans // lon_n), :]
                    w1_send[which, d, 3 * a + b] = part.astype(BF)
        copies = []
        for step in range(1, lon_n):
            copy = remote(
                w1_send.at[which, lon_id(step)], w1_recv.at[which, step - 1],
                w1_s.at[which, step - 1], w1_r.at[which, step - 1], {"lon": lon_id(step)},
            )
            copy.start()
            copies.append(copy)
        return copies

    def over_frames(which, copies):
        part = chans // lon_n
        total = grads[which, :, pl.ds(pl.multiple_of(lon * part, part), part), :]
        for step in range(1, lon_n):
            copies[step - 1].wait()
            total = total + w1_recv[which, step - 1].astype(F32)
        if chunk * frame_n > 9 * part:
            acc[...] = jnp.zeros_like(acc)
        acc[0 : 9 * part, :] = total.reshape(9 * part, chans)
        for f in range(frame_n):
            piece = acc[f * chunk : (f + 1) * chunk, :]
            w2_own[which, f] = piece
            w2_send[which, f] = piece.astype(BF)
        out = []
        for step in range(1, frame_n):
            copy = remote(
                w2_send.at[which, frame_id(step)], w2_recv.at[which, step - 1],
                w2_s.at[which, step - 1], w2_r.at[which, step - 1], {"frame": frame_id(step)},
            )
            copy.start()
            out.append(copy)
        return out

    def gather_frames(which, copies):
        total = w2_own[which, frame]
        for step in range(1, frame_n):
            copies[step - 1].wait()
            total = total + w2_recv[which, step - 1].astype(F32)
        ag1[which, 0] = total.astype(BF)
        out = []
        for step in range(1, frame_n):
            copy = remote(
                ag1.at[which, 0], ag1.at[which, step],
                a1_s.at[which, step - 1], a1_r.at[which, step - 1], {"frame": frame_id(step)},
            )
            copy.start()
            out.append(copy)
        return out

    def gather_lon(which, copies):
        for copy in copies:
            copy.wait()
        out = []
        for step in range(1, lon_n):
            copy = remote(
                ag1.at[which], ag2.at[which, step - 1],
                a2_s.at[which, step - 1], a2_r.at[which, step - 1], {"lon": lon_id(step)},
            )
            copy.start()
            out.append(copy)
        return out

    def finish(which, copies, out):
        part = chans // lon_n
        for step in range(lon_n):
            if step:
                copies[step - 1].wait()
            for f in range(frame_n):
                if step:
                    piece = ag2[which, step - 1, f]
                else:
                    piece = ag1[which, f]
                wide_out[frame_id(-f)] = piece.astype(F32)
            for f in range(frame_n):
                acc[f * chunk : (f + 1) * chunk, :] = wide_out[f]
            out[lon_id(-step)] = acc[0 : 9 * part, :].reshape(9, part, chans).astype(BF)

    for g in range(2):
        block = gext[1 + g * half : 1 + (g + 1) * half, 8 : 8 + WIDE, :]
        block = jnp.where(inside, block, 0.0).reshape(half * WIDE, chans)
        gt[:, g * half * WIDE : (g + 1) * half * WIDE] = block.T.astype(BF)
    second1 = weight_terms(0, xh)

    for g in range(2):
        back = conv(xg, wb, g * half).reshape(half, WIDE, chans)
        active = hext[1 + g * half : 1 + (g + 1) * half, 8 : 8 + WIDE, :] > 0
        block = jnp.where(active & inside, back, 0.0).reshape(half * WIDE, chans)
        gt[:, g * half * WIDE : (g + 1) * half * WIDE] = block.T.astype(BF)
    first1 = weight_terms(1, xx)
    second2 = over_frames(0, second1)

    for step in range(1, lon_n):
        returns[step - 1].wait()
        retall[:, step * cap : (step + 1) * cap] = ret_recv[step - 1]
    home = dot(retall[...], pt[...]).T
    share = tracks // frame_n
    for f in range(frame_n):
        piece = home[f * share : (f + 1) * share, :]
        qg_own[f] = piece
        qg_send[f] = piece.astype(BF)
    qgs = []
    for step in range(1, frame_n):
        copy = remote(
            qg_send.at[frame_id(step)], qg_recv.at[step - 1], qg_s.at[step - 1],
            qg_r.at[step - 1], {"frame": frame_id(step)},
        )
        copy.start()
        qgs.append(copy)

    first2 = over_frames(1, first1)
    second3 = gather_frames(0, second2)
    first3 = gather_frames(1, first2)
    second4 = gather_lon(0, second3)
    total = qg_own[frame]
    for step in range(1, frame_n):
        qgs[step - 1].wait()
        total = total + qg_recv[step - 1].astype(F32)
    query_out[...] = total
    first4 = gather_lon(1, first3)
    finish(0, second4, second_out)
    finish(1, first4, first_out)


def per_device(
    layer_input, hidden_saved, conv_weight, queries, corr_cotangent,
    window_rows, window_cols, owner_strip,
):
    lon_n, frame_n = lax.axis_size("lon"), lax.axis_size("frame")
    _, rows_n, cols_n, chans = hidden_saved.shape
    tracks = queries.shape[0]
    cap = tracks // 4
    slots = lon_n * cap
    part = chans // lon_n
    chunk = -(-9 * part // frame_n)
    scale = 1.0 / math.sqrt(rows_n * cols_n * lon_n * frame_n)
    dims = (lon_n, frame_n, rows_n, cols_n, chans, tracks, cap, chunk, scale)
    share = tracks // frame_n
    vm = pltpu.VMEM
    dma = pltpu.SemaphoreType.DMA
    scratch = [
        vm((rows_n + 2, EXT, chans), F32),
        vm((rows_n + 2, EXT, chans), F32),
        vm((rows_n + 2, EXT, chans), F32),
        vm((rows_n + 2, WIDE, 3 * chans), BF),
        vm((rows_n + 2, WIDE, 3 * chans), BF),
        vm((rows_n + 2, WIDE, 3 * chans), BF),
        vm((rows_n * WIDE, chans), BF),
        vm((3, 3 * chans, chans), BF),
        vm((rows_n, WIDE, chans), F32),
        vm((chans, rows_n * WIDE), BF),
        vm((rows_n * WIDE, slots), BF),
        vm((64, tracks), F32),
        vm((slots, tracks), BF),
        vm((slots, chans), BF),
        vm((64, slots), F32),
        vm((lon_n - 1, cap + 64, chans), BF),
        vm((lon_n - 1, cap + 64, chans), BF),
        vm((2, rows_n, 8, chans), BF),
        vm((2, rows_n, 8, chans), BF),
        vm((2, rows_n, 8, chans), F32),
        vm((2, rows_n, 8, chans), F32),
        vm((lon_n - 1, chans, cap), BF),
        vm((lon_n - 1, chans, cap), BF),
        vm((chans, slots), BF),
        vm((frame_n, share, chans), BF),
        vm((frame_n, share, chans), F32),
        vm((frame_n - 1, share, chans), BF),
        vm((2, 9, chans, chans), F32),
        vm((2, lon_n, 9, part, chans), BF),
        vm((2, lon_n - 1, 9, part, chans), BF),
        vm((chunk * frame_n, chans), F32),
        vm((2, frame_n, chunk, chans), F32),
        vm((2, frame_n, chunk, chans), BF),
        vm((2, frame_n - 1, chunk, chans), BF),
        vm((2, frame_n, chunk, chans), BF),
        vm((2, lon_n - 1, frame_n, chunk, chans), BF),
        vm((frame_n, chunk, chans), F32),
        dma((lon_n - 1,)), dma((lon_n - 1,)),
        dma((2,)), dma((2,)),
        dma((2,)), dma((2,)),
        dma((lon_n - 1,)), dma((lon_n - 1,)),
        dma((frame_n - 1,)), dma((frame_n - 1,)),
        dma((2, lon_n - 1)), dma((2, lon_n - 1)),
        dma((2, frame_n - 1)), dma((2, frame_n - 1)),
        dma((2, frame_n - 1)), dma((2, frame_n - 1)),
        dma((2, lon_n - 1)), dma((2, lon_n - 1)),
    ]
    spec = pl.BlockSpec(memory_space=pltpu.VMEM)
    query_grad, first, second = pl.pallas_call(
        functools.partial(kernel, dims),
        out_shape=(
            jax.ShapeDtypeStruct((share, chans), F32),
            jax.ShapeDtypeStruct((lon_n, 9, part, chans), BF),
            jax.ShapeDtypeStruct((lon_n, 9, part, chans), BF),
        ),
        in_specs=[spec] * 8,
        out_specs=(spec,) * 3,
        scratch_shapes=scratch,
        compiler_params=pltpu.CompilerParams(
            collective_id=0, has_side_effects=True, vmem_limit_bytes=60 * 1024 * 1024
        ),
    )(
        layer_input[0], hidden_saved[0], conv_weight.reshape(3, 3 * chans, chans), queries,
        corr_cotangent[0], window_rows, window_cols, owner_strip[:, :, 0],
    )

    def unfold(value):
        return value.transpose(1, 0, 2, 3).reshape(3, 3, chans, chans).astype(F32)

    return query_grad, unfold(first), unfold(second)


def solution(mesh):
    placed = (
        P("frame", None, "lon", None),
        P("frame", None, "lon", None),
        P(),
        P("lon", None),
        P("frame", None, "lon"),
        P("frame", "lon"),
        P("frame", "lon"),
        P("frame", "lon", None),
    )
    return jax.shard_map(
        per_device,
        mesh=mesh,
        in_specs=placed,
        out_specs=(P(("lon", "frame"), None), P(), P()),
        check_vma=False,
    )
```

profile of v0, /device:TPU:0, one launch (start us, length us, event | category | flops | bytes accessed | tf_op | source)
XLA Modules:
  0.0 48.3 jit_solution(10278073476781288606)
XLA Ops:
  0.6 44.1 %shard_map.103 = (f32[64,128]{1,0:T(8,128)}, bf16[4,9,32,128]{3,2,1,0:T(8,128)(2,1)}, bf16[4,9,32,128]{3,2,1,0:T(8,128)(2,1)}) custom-call(bf16[16,128,128]{2,1,0:T(8,128)(2,1)} %bitcast.13, bf16[16,128,128]{2,1,0:T(8,128)(2,1)} %bitcast.14, bf16[3,384,128]{2,1,0:T(8,128)(2,1)} %bitcast.15, bf16[512,128]{1,0:T(8,128)(2,1)} %q_ref.1, ...), custom_call_target="tpu_custom_call" | custom-call | tf_op jit(solution)/shard_map/pallas_call | solution.py:421
  44.8 1.2 %convert_bitcast_fusion = (f32[9,4,32,128]{3,2,0,1:T(8,128)S(1)}, f32[9,4,32,128]{3,2,0,1:T(8,128)S(1)}) fusion(bf16[4,9,32,128]{3,2,1,0:T(8,128)(2,1)} %get-tuple-element.8, bf16[4,9,32,128]{3,2,1,0:T(8,128)(2,1)} %get-tuple-element.7), kind=kLoop, calls=%fused_computation | loop fusion | flops 294912 | bytes 1769472 | tf_op jit(solution)/shard_map/convert_element_type | solution.py:440
  46.0 0.9 %copy.12 = f32[9,4,32,128]{3,2,1,0:T(8,128)} copy(f32[9,4,32,128]{3,2,0,1:T(8,128)S(1)} %get-tuple-element.9) | data formatting | bytes 1179648 | tf_op jit(solution)/shard_map/convert_element_type | solution.py:440
  46.8 0.0 copy-start
  46.8 0.9 %copy.11 = f32[9,4,32,128]{3,2,1,0:T(8,128)} copy(f32[9,4,32,128]{3,2,0,1:T(8,128)S(1)} %get-tuple-element.10) | data formatting | bytes 1179648 | tf_op jit(solution)/shard_map/convert_element_type | solution.py:440
  47.7 0.0 copy-done
  47.7 0.6 %copy.14 = f32[64,128]{1,0:T(8,128)} copy(f32[64,128]{1,0:T(8,128)S(1)} %copy-done) | data formatting | bytes 65536
Async XLA Ops:
  46.8 0.9 %copy-start = (f32[64,128]{1,0:T(8,128)S(1)}, f32[64,128]{1,0:T(8,128)}, u32[]{:S(2)}) copy-start(f32[64,128]{1,0:T(8,128)} %get-tuple-element.14) | copy-start | bytes 98308
where the time goes:
time: 49 us; the launch traced here: 48.3 us
  Pallas kernels  44.1 us (90%)
  local copies, waits for them, and re-layouts  2.35 us (5%)
  other arithmetic  1.19 us (2%)
  between operations  0.65 us (1%)
    pallas_call x1, Pallas kernels, per_device(): pl.pallas_call(functools.partial(kernel, dims), out_shape=(jax.ShapeDtype...  44.1 us
    convert_element_type x2, local copies, waits for them, and re-layouts, unfold(): return value.transpose(1, 0, 2, 3).reshape(3, 3, chans, chans).astype(F32)  1.73 us
    convert_element_type x1, other arithmetic, unfold(): return value.transpose(1, 0, 2, 3).reshape(3, 3, chans, chans).astype(F32)  1.19 us

commit v1 on v0

v1 whole, which is shorter than its diff:
```python
import functools
import math

import jax
import jax.numpy as jnp
from jax import lax
from jax.experimental import pallas as pl
from jax.experimental.pallas import tpu as pltpu
from jax.sharding import PartitionSpec as P

WIN = 7
WIDE = 144
EXT = 160
BF = jnp.bfloat16
F32 = jnp.float32
MESH = pl.DeviceIdType.MESH
HALO = 9
UNROLL = 32


def dot(a, b):
    return jnp.dot(a, b, preferred_element_type=F32)


def each(count, body):
    if count <= UNROLL:
        for s in range(count):
            body(s)
    else:
        pl.loop(0, count)(body)


def kernel(
    dims,
    x_ref, h_ref, w_ref, q_ref, cot_ref, rows_ref, cols_ref, own_ref,
    query_out, first_out, second_out,
    hext, xext, gext, xh, xx, xg, feat, wb, gt, spread,
    cm, pt, qall, cmall,
    pay_send, pay_recv, strip, halo_send, halo_recv,
    ret_send, ret_recv, retall, qg_send, qg_own, qg_recv,
    grads, half_send, half_recv, acc, rs_send, rs_recv, ag,
    pay_s, pay_r, halo_s, halo_r, ret_s, ret_r, qg_s, qg_r,
    half_s, half_r, rs_s, rs_r, ag_s, ag_r, pair_s, pair_r,
):
    lon_n, frame_n, rows_n, cols_n, chans, tracks, cap, group_n, chunk, scale = dims
    lon, frame = lax.axis_index("lon"), lax.axis_index("frame")
    slots = lon_n * cap
    half = rows_n // 2
    core = lax.rem(lon, 2)
    place = (lon // 2) * frame_n + frame
    part = 9 * chans // 2

    def lon_id(steps):
        return lax.rem(lon + steps + lon_n, lon_n)

    def frame_id(steps):
        return lax.rem(frame + steps + frame_n, frame_n)

    def group_id(steps):
        return lax.rem(place + steps, group_n)

    def group_device(p):
        return {"lon": (p // frame_n) * 2 + core, "frame": lax.rem(p, frame_n)}

    pair = {"lon": lon + 1 - 2 * core}

    def remote(src, dst, send, recv, where):
        return pltpu.make_async_remote_copy(
            src_ref=src, dst_ref=dst, send_sem=send, recv_sem=recv,
            device_id=where, device_id_type=MESH,
        )

    barrier = pltpu.get_barrier_semaphore()
    for step in range(1, lon_n):
        pl.semaphore_signal(barrier, inc=1, device_id={"lon": lon_id(step)}, device_id_type=MESH)

    def greet(s):
        pl.semaphore_signal(
            barrier, inc=1, device_id=group_device(group_id(s + 1)), device_id_type=MESH
        )

    each(group_n - 1, greet)

    for side in range(2):
        edge = cols_n - 8 if side == 0 else 0
        h_edge = h_ref[:, edge : edge + 8].astype(F32)
        x_edge = x_ref[:, edge : edge + 8].astype(F32)
        for r in range(rows_n):
            if side == 0:
                strip[HALO * r : HALO * r + 4, :] = h_edge[r, 4:8]
                strip[HALO * r + 4 : HALO * r + 9, :] = x_edge[r, 3:8]
            else:
                strip[HALO * r : HALO * r + 4, :] = h_edge[r, 0:4]
                strip[HALO * r + 4 : HALO * r + 9, :] = x_edge[r, 0:5]
        halo_send[side] = strip[...].astype(BF)

    owners = own_ref[...]
    marks = (owners == lax.broadcasted_iota(jnp.int32, (16, tracks), 0)).astype(F32)
    earlier = (
        lax.broadcasted_iota(jnp.int32, (tracks, tracks), 0)
        < lax.broadcasted_iota(jnp.int32, (tracks, tracks), 1)
    ).astype(F32).astype(BF)
    before = dot(marks.astype(BF), earlier)
    rank = jnp.sum(before * marks, axis=0, keepdims=True).astype(jnp.int32)
    slot = owners * cap + rank
    cm[...] = jnp.zeros_like(cm)
    for i in range(WIN):
        cm[8 * i : 8 * i + WIN, :] = cot_ref[WIN * i : WIN * i + WIN, :].astype(F32)
    cm[56:57, :] = rows_ref[...].astype(F32)
    cm[57:58, :] = (cols_ref[...] + 3).astype(F32)
    cm_half = cm[...].astype(BF)

    pays = []
    for step in list(range(1, lon_n)) + [0]:
        local = slot - lon_id(step) * cap
        hot = (local == lax.broadcasted_iota(jnp.int32, (cap, tracks), 0)).astype(F32).astype(BF)
        pt[step * cap : (step + 1) * cap, :] = hot
        q_part = dot(hot, q_ref[...]).astype(BF)
        c_part = lax.dot_general(
            cm_half, hot, (((1,), (1,)), ((), ())), preferred_element_type=F32
        )
        if step:
            pay_send[step - 1, 0:cap, :] = q_part
            pay_send[step - 1, cap : cap + 64, :] = c_part.astype(BF)
        else:
            qall[0:cap, :] = q_part
            cmall[:, 0:cap] = c_part

    pl.semaphore_wait(barrier, lon_n - 1 + group_n - 1)
    for step in range(1, lon_n):
        copy = remote(
            pay_send.at[step - 1], pay_recv.at[step - 1], pay_s.at[step - 1],
            pay_r.at[step - 1], {"lon": lon_id(step)},
        )
        copy.start()
        pays.append(copy)
    halos = [
        remote(halo_send.at[0], halo_recv.at[0], halo_s.at[0], halo_r.at[0], {"lon": lon_id(1)}),
        remote(halo_send.at[1], halo_recv.at[1], halo_s.at[1], halo_r.at[1], {"lon": lon_id(-1)}),
    ]
    for copy in halos:
        copy.start()

    for a in range(3):
        for b in range(3):
            tap = w_ref[2 - a, (2 - b) * chans : (3 - b) * chans, :].astype(F32)
            wb[a, b * chans : (b + 1) * chans, :] = tap.T.astype(BF)

    def fill(ext, src):
        ext[...] = jnp.zeros_like(ext)

        @pl.loop(0, rows_n)
        def _(r):
            ext[r + 1, 16 : 16 + cols_n, :] = src[r].astype(F32)

    def side_by_side(ext, out):
        @pl.loop(0, rows_n + 2)
        def _(r):
            for b in range(3):
                out[r, :, b * chans : (b + 1) * chans] = ext[r, 7 + b : 7 + b + WIDE, :].astype(BF)

    def conv(source, weight, r0):
        total = None
        for a in range(3):
            block = source[r0 + a : r0 + a + half].reshape(half * WIDE, 3 * chans)
            term = dot(block, weight[a])
            total = term if total is None else total + term
        return total

    def spread_block(step):
        lanes = slice(step * cap, (step + 1) * cap)
        rows_t = cmall[56:57, lanes].astype(jnp.int32)
        cols_t = cmall[57:58, lanes].astype(jnp.int32) + 5
        placed = []
        for r in range(rows_n):
            value = jnp.zeros((8, cap), F32)
            for i in range(WIN):
                if 0 <= r - i <= rows_n - WIN:
                    value = jnp.where(rows_t == r - i, cmall[8 * i : 8 * i + 8, lanes], value)
            placed.append(value)

        @pl.loop(0, WIDE // 16)
        def _(tile):
            offset = lax.broadcasted_iota(jnp.int32, (16, cap), 0) + tile * 16 - cols_t
            hits = [offset == j for j in range(WIN)]
            for r in range(rows_n):
                value = jnp.zeros((16, cap), F32)
                for j in range(WIN):
                    value = jnp.where(hits[j], placed[r][j : j + 1, :], value)
                start = pl.multiple_of(r * WIDE + tile * 16, 16)
                spread[pl.ds(start, 16), lanes] = value.astype(BF)

    fill(hext, h_ref)
    fill(xext, x_ref)
    gext[...] = jnp.zeros_like(gext)
    spread_block(0)

    for step in range(1, lon_n):
        pays[step - 1].wait()
        qall[step * cap : (step + 1) * cap, :] = pay_recv[step - 1, 0:cap, :]
        cmall[:, step * cap : (step + 1) * cap] = pay_recv[step - 1, cap : cap + 64, :].astype(F32)
        spread_block(step)

    for side in range(2):
        halos[side].wait()
        strip[...] = halo_recv[side].astype(F32)
        for r in range(rows_n):
            h_edge = strip[HALO * r : HALO * r + 4, :]
            x_edge = strip[HALO * r + 4 : HALO * r + 9, :]
            if side == 0:
                hext[r + 1, 12:16, :] = h_edge
                xext[r + 1, 11:16, :] = x_edge
            else:
                hext[r + 1, 16 + cols_n : 20 + cols_n, :] = h_edge
                xext[r + 1, 16 + cols_n : 21 + cols_n, :] = x_edge
    side_by_side(hext, xh)

    for g in range(2):
        cells = slice(g * half * WIDE, (g + 1) * half * WIDE)
        block = dot(spread[cells, :], qall[...])
        gext[1 + g * half : 1 + (g + 1) * half, 8 : 8 + WIDE, :] = block.reshape(half, WIDE, chans)
        gt[:, g * half * WIDE : (g + 1) * half * WIDE] = block.T.astype(BF)

    def halves(which):
        return remote(
            half_send.at[which], half_recv.at[which], half_s.at[which], half_r.at[which], pair
        )

    def scatter(which, s):
        p = group_id(s + 1)
        return remote(
            rs_send.at[which, p], rs_recv.at[which, s], rs_s.at[which, s], rs_r.at[which, s],
            group_device(p),
        )

    def gather(which, s):
        return remote(
            ag.at[which, place], ag.at[which, place], ag_s.at[which, s], ag_r.at[which, s],
            group_device(group_id(s + 1)),
        )

    outs = (second_out, first_out)

    def pairs(which):
        return remote(
            ag.at[which], outs[which].at[core], pair_s.at[which], pair_r.at[which], pair
        )

    def weight_terms(which, source):
        for a in range(3):
            block = source[a : a + rows_n].reshape(rows_n * WIDE, 3 * chans)
            term = dot(gt[...], block) * scale
            for b in range(3):
                row = (3 * a + b) * chans
                grads[which, row : row + chans, :] = term[:, b * chans : (b + 1) * chans].T
        other = pl.ds(pl.multiple_of((1 - core) * part, 8), part)
        half_send[which] = grads[which, other, :].astype(BF)
        halves(which).start()

    def scatter_start(which):
        halves(which).wait()
        mine = pl.ds(pl.multiple_of(core * part, 8), part)
        if group_n * chunk > part:
            acc[part:, :] = jnp.zeros((group_n * chunk - part, chans), F32)
        acc[0:part, :] = grads[which, mine, :] + half_recv[which].astype(F32)
        for p in range(group_n):
            rs_send[which, p] = acc[p * chunk : (p + 1) * chunk, :].astype(BF)
        each(group_n - 1, lambda s: scatter(which, s).start())

    def gather_start(which):
        total = rs_send[which, place].astype(F32)
        if group_n - 1 <= UNROLL:
            for s in range(group_n - 1):
                scatter(which, s).wait()
                total = total + rs_recv[which, s].astype(F32)
        else:
            def add(s, value):
                scatter(which, s).wait()
                return value + rs_recv[which, s].astype(F32)

            total = lax.fori_loop(0, group_n - 1, add, total)
        ag[which, place] = total.astype(BF)
        each(group_n - 1, lambda s: gather(which, s).start())

    def pair_start(which):
        each(group_n - 1, lambda s: gather(which, s).wait())
        pairs(which).start()
        outs[which][core] = ag[which]

    weight_terms(0, xh)

    for g in range(2):
        feat[g * half * WIDE : (g + 1) * half * WIDE, :] = conv(xh, w_ref, g * half).astype(BF)
    slot_grads = lax.dot_general(
        feat[...], spread[...], (((0,), (0,)), ((), ())), preferred_element_type=F32
    )
    retall[:, 0:cap] = slot_grads[:, 0:cap].astype(BF)
    returns = []
    for step in range(1, lon_n):
        ret_send[step - 1] = slot_grads[:, step * cap : (step + 1) * cap].astype(BF)
        copy = remote(
            ret_send.at[step - 1], ret_recv.at[step - 1], ret_s.at[step - 1],
            ret_r.at[step - 1], {"lon": lon_id(-step)},
        )
        copy.start()
        returns.append(copy)

    scatter_start(0)
    side_by_side(gext, xg)
    side_by_side(xext, xx)
    for g in range(2):
        back = conv(xg, wb, g * half).reshape(half, WIDE, chans)
        active = hext[1 + g * half : 1 + (g + 1) * half, 8 : 8 + WIDE, :] > 0
        block = jnp.where(active, back, 0.0).reshape(half * WIDE, chans)
        gt[:, g * half * WIDE : (g + 1) * half * WIDE] = block.T.astype(BF)
    weight_terms(1, xx)

    scatter_start(1)
    for step in range(1, lon_n):
        returns[step - 1].wait()
        retall[:, step * cap : (step + 1) * cap] = ret_recv[step - 1]
    home = dot(retall[...], pt[...]).T
    share = tracks // frame_n
    for f in range(frame_n):
        piece = home[f * share : (f + 1) * share, :]
        qg_own[f] = piece
        qg_send[f] = piece.astype(BF)
    qgs = []
    for step in range(1, frame_n):
        copy = remote(
            qg_send.at[frame_id(step)], qg_recv.at[step - 1], qg_s.at[step - 1],
            qg_r.at[step - 1], {"frame": frame_id(step)},
        )
        copy.start()
        qgs.append(copy)

    gather_start(0)
    gather_start(1)
    pair_start(0)
    total = qg_own[frame]
    for step in range(1, frame_n):
        qgs[step - 1].wait()
        total = total + qg_recv[step - 1].astype(F32)
    query_out[...] = total
    pair_start(1)
    pairs(0).wait()
    pairs(1).wait()


def expand(dims, query_ref, first_ref, second_ref, query_out, first_out, second_out):
    part, group_n, chunk = dims
    query_out[...] = query_ref[...]
    for source, out in ((first_ref, first_out), (second_ref, second_out)):
        for c in range(2):
            for p in range(group_n):
                rows = min(chunk, part - p * chunk)
                if rows > 0:
                    start = c * part + p * chunk
                    out[start : start + rows, :] = source[c, p].astype(F32)[0:rows]


def per_device(
    layer_input, hidden_saved, conv_weight, queries, corr_cotangent,
    window_rows, window_cols, owner_strip,
):
    lon_n, frame_n = lax.axis_size("lon"), lax.axis_size("frame")
    _, rows_n, cols_n, chans = hidden_saved.shape
    tracks = queries.shape[0]
    cap = tracks // 4
    slots = lon_n * cap
    part = 9 * chans // 2
    group_n = lon_n // 2 * frame_n
    chunk = -(-part // group_n)
    scale = 1.0 / math.sqrt(rows_n * cols_n * lon_n * frame_n)
    dims = (lon_n, frame_n, rows_n, cols_n, chans, tracks, cap, group_n, chunk, scale)
    share = tracks // frame_n
    vm = pltpu.VMEM
    dma = pltpu.SemaphoreType.DMA
    scratch = [
        vm((rows_n + 2, EXT, chans), F32),
        vm((rows_n + 2, EXT, chans), F32),
        vm((rows_n + 2, EXT, chans), F32),
        vm((rows_n + 2, WIDE, 3 * chans), BF),
        vm((rows_n + 2, WIDE, 3 * chans), BF),
        vm((rows_n + 2, WIDE, 3 * chans), BF),
        vm((rows_n * WIDE, chans), BF),
        vm((3, 3 * chans, chans), BF),
        vm((chans, rows_n * WIDE), BF),
        vm((rows_n * WIDE, slots), BF),
        vm((64, tracks), F32),
        vm((slots, tracks), BF),
        vm((slots, chans), BF),
        vm((64, slots), F32),
        vm((lon_n - 1, cap + 64, chans), BF),
        vm((lon_n - 1, cap + 64, chans), BF),
        vm((HALO * rows_n, chans), F32),
        vm((2, HALO * rows_n, chans), BF),
        vm((2, HALO * rows_n, chans), BF),
        vm((lon_n - 1, chans, cap), BF),
        vm((lon_n - 1, chans, cap), BF),
        vm((chans, slots), BF),
        vm((frame_n, share, chans), BF),
        vm((frame_n, share, chans), F32),
        vm((frame_n - 1, share, chans), BF),
        vm((2, 9 * chans, chans), F32),
        vm((2, part, chans), BF),
        vm((2, part, chans), BF),
        vm((group_n * chunk, chans), F32),
        vm((2, group_n, chunk, chans), BF),
        vm((2, group_n - 1, chunk, chans), BF),
        vm((2, group_n, chunk, chans), BF),
        dma((lon_n - 1,)), dma((lon_n - 1,)),
        dma((2,)), dma((2,)),
        dma((lon_n - 1,)), dma((lon_n - 1,)),
        dma((frame_n - 1,)), dma((frame_n - 1,)),
        dma((2,)), dma((2,)),
        dma((2, group_n - 1)), dma((2, group_n - 1)),
        dma((2, group_n - 1)), dma((2, group_n - 1)),
        dma((2,)), dma((2,)),
    ]
    spec = pl.BlockSpec(memory_space=pltpu.VMEM)
    gathered = jax.ShapeDtypeStruct((2, group_n, chunk, chans), BF)
    query_grad, first, second = pl.pallas_call(
        functools.partial(kernel, dims),
        out_shape=(jax.ShapeDtypeStruct((share, chans), F32), gathered, gathered),
        in_specs=[spec] * 8,
        out_specs=(spec,) * 3,
        scratch_shapes=scratch,
        compiler_params=pltpu.CompilerParams(
            collective_id=0, has_side_effects=True, vmem_limit_bytes=60 * 1024 * 1024
        ),
    )(
        layer_input[0], hidden_saved[0], conv_weight.reshape(3, 3 * chans, chans), queries,
        corr_cotangent[0], window_rows, window_cols, owner_strip[:, :, 0],
    )
    weight = jax.ShapeDtypeStruct((9 * chans, chans), F32)
    query_grad, first, second = pl.pallas_call(
        functools.partial(expand, (part, group_n, chunk)),
        out_shape=(jax.ShapeDtypeStruct((share, chans), F32), weight, weight),
        in_specs=[spec] * 3,
        out_specs=(spec,) * 3,
    )(query_grad, first, second)
    return (
        query_grad,
        first.reshape(3, 3, chans, chans),
        second.reshape(3, 3, chans, chans),
    )


def solution(mesh):
    placed = (
        P("frame", None, "lon", None),
        P("frame", None, "lon", None),
        P(),
        P("lon", None),
        P("frame", None, "lon"),
        P("frame", "lon"),
        P("frame", "lon"),
        P("frame", "lon", None),
    )
    return jax.shard_map(
        per_device,
        mesh=mesh,
        in_specs=placed,
        out_specs=(P(("lon", "frame"), None), P(), P()),
        check_vma=False,
    )
```

time: 49 us -> 42.3 us (0.86)
  Pallas kernels: 44.1 us -> 41.5 us
  local copies, waits for them, and re-layouts: 2.35 us -> 0 us
  other arithmetic: 1.19 us -> 0 us
    pallas_call x1, Pallas kernels: 44.1 us -> 39.3 us  [per_device(): pl.pallas_call(functools.partial(kernel, dims), out_shape=(jax.ShapeDtype...]
    pallas_call x0 -> x1, Pallas kernels: none -> 2.14 us  [per_device(): pl.pallas_call(functools.partial(expand, (part, group_n, chunk)), out_sha...]
    convert_element_type x2 -> x0, local copies, waits for them, and re-layouts: 1.73 us -> none  [unfold(): return value.transpose(1, 0, 2, 3).reshape(3, 3, chans, chans).astype(F32)]
    convert_element_type x1 -> x0, other arithmetic: 1.19 us -> none  [unfold(): return value.transpose(1, 0, 2, 3).reshape(3, 3, chans, chans).astype(F32)]
    unnamed x3 -> x0, local copies, waits for them, and re-layouts: 0.62 us -> none
where the time goes in v1:
time: 42.3 us; the launch traced here: 42.1 us
  Pallas kernels  41.5 us (98%)
  between operations  0.64 us (2%)
    pallas_call x1, Pallas kernels, per_device(): pl.pallas_call(functools.partial(kernel, dims), out_shape=(jax.ShapeDtype...  39.3 us
    pallas_call x1, Pallas kernels, per_device(): pl.pallas_call(functools.partial(expand, (part, group_n, chunk)), out_sha...  2.14 us

profile of v1, /device:TPU:0, one launch (start us, length us, event | category | flops | bytes accessed | tf_op | source)
XLA Modules:
  0.0 42.1 jit_solution(7379975552695940988)
XLA Ops:
  0.6 39.3 %shard_map.103 = (f32[64,128]{1,0:T(8,128)}, bf16[2,16,36,128]{3,2,1,0:T(8,128)(2,1)}, bf16[2,16,36,128]{3,2,1,0:T(8,128)(2,1)}) custom-call(bf16[16,128,128]{2,1,0:T(8,128)(2,1)} %bitcast.7, bf16[16,128,128]{2,1,0:T(8,128)(2,1)} %bitcast.8, bf16[3,384,128]{2,1,0:T(8,128)(2,1)} %bitcast.9, bf16[512,128]{1,0:T(8,128)(2,1)} %q_ref.1, ...), custom_call_target="tpu_custom_call" | custom-call | tf_op jit(solution)/shard_map/pallas_call | solution.py:423
  40.0 2.1 %shard_map.104 = (f32[64,128]{1,0:T(8,128)}, f32[1152,128]{1,0:T(8,128)}, f32[1152,128]{1,0:T(8,128)}) custom-call(f32[64,128]{1,0:T(8,128)} %get-tuple-element.9.query_ref, bf16[2,16,36,128]{3,2,1,0:T(8,128)(2,1)} %get-tuple-element.10.first_ref, bf16[2,16,36,128]{3,2,1,0:T(8,128)(2,1)} %get-tuple-element.11.second_ref), custom_call_target="tpu_custom_call" | custom-call | tf_op jit(solution)/shard_map/pallas_call | solution.py:437

commit v2 on v1

--- a/solution.py
+++ b/solution.py
@@ -9,12 +9,13 @@
 from jax.sharding import PartitionSpec as P
 
 WIN = 7
-WIDE = 144
+EDGE = 16
 EXT = 160
 BF = jnp.bfloat16
 F32 = jnp.float32
 MESH = pl.DeviceIdType.MESH
 HALO = 9
+BAND = 4
 UNROLL = 32
 
 
@@ -34,7 +35,7 @@
     dims,
     x_ref, h_ref, w_ref, q_ref, cot_ref, rows_ref, cols_ref, own_ref,
     query_out, first_out, second_out,
-    hext, xext, gext, xh, xx, xg, feat, wb, gt, spread,
+    hext, gext, pext, xh, xhm, xg, xgm, xp, xpm, feat_t, wb, ht, xt, spread, edge,
     cm, pt, qall, cmall,
     pay_send, pay_recv, strip, halo_send, halo_recv,
     ret_send, ret_recv, retall, qg_send, qg_own, qg_recv,
@@ -82,9 +83,9 @@
     each(group_n - 1, greet)
 
     for side in range(2):
-        edge = cols_n - 8 if side == 0 else 0
-        h_edge = h_ref[:, edge : edge + 8].astype(F32)
-        x_edge = x_ref[:, edge : edge + 8].astype(F32)
+        first = cols_n - 8 if side == 0 else 0
+        h_edge = h_ref[:, first : first + 8].astype(F32)
+        x_edge = x_ref[:, first : first + 8].astype(F32)
         for r in range(rows_n):
             if side == 0:
                 strip[HALO * r : HALO * r + 4, :] = h_edge[r, 4:8]
@@ -143,34 +144,53 @@
 
     for a in range(3):
         for b in range(3):
-            tap = w_ref[2 - a, (2 - b) * chans : (3 - b) * chans, :].astype(F32)
+            tap = w_ref[2 - a, b * chans : (b + 1) * chans, :].astype(F32)
             wb[a, b * chans : (b + 1) * chans, :] = tap.T.astype(BF)
 
-    def fill(ext, src):
-        ext[...] = jnp.zeros_like(ext)
-
-        @pl.loop(0, rows_n)
-        def _(r):
-            ext[r + 1, 16 : 16 + cols_n, :] = src[r].astype(F32)
-
-    def side_by_side(ext, out):
-        @pl.loop(0, rows_n + 2)
-        def _(r):
+    cells, rim = rows_n * cols_n, rows_n * EDGE
+
+    def turned(src, out):
+        out[0:chans, 0:cols_n] = jnp.zeros((chans, cols_n), BF)
+        out[2 * chans : 3 * chans, cells - cols_n : cells] = jnp.zeros((chans, cols_n), BF)
+        for r in range(rows_n):
+            tile = src[r].astype(F32).T.astype(BF)
+            for a in range(3):
+                if 0 <= r + 1 - a < rows_n:
+                    at = (r + 1 - a) * cols_n
+                    out[a * chans : (a + 1) * chans, at : at + cols_n] = tile
+
+    def turned_edge(out):
+        for a in range(3):
+            block = edge[a : a + rows_n].reshape(rim, chans)
+            out[a * chans : (a + 1) * chans, cells : cells + rim] = block.T.astype(BF)
+
+    def side_by_side(ext, out, out_edge, flip):
+        for r in range(1, rows_n + 1):
+            at, low = r * cols_n, r * EDGE
             for b in range(3):
-                out[r, :, b * chans : (b + 1) * chans] = ext[r, 7 + b : 7 + b + WIDE, :].astype(BF)
-
-    def conv(source, weight, r0):
+                by = 1 - b if flip else b - 1
+                lanes = slice(b * chans, (b + 1) * chans)
+                out[pl.ds(at, cols_n), lanes] = ext[r, 16 + by : 16 + by + cols_n, :].astype(BF)
+                rim_cells = jnp.concatenate(
+                    [
+                        ext[r, 8 + by : 16 + by, :],
+                        ext[r, 16 + cols_n + by : 24 + cols_n + by, :],
+                    ],
+                    axis=0,
+                )
+                out_edge[pl.ds(low, EDGE), lanes] = rim_cells.astype(BF)
+
+    def conv(source, weight, start, count, step):
         total = None
         for a in range(3):
-            block = source[r0 + a : r0 + a + half].reshape(half * WIDE, 3 * chans)
-            term = dot(block, weight[a])
+            term = dot(source[pl.ds(start + a * step, count), :], weight[a])
             total = term if total is None else total + term
         return total
 
     def spread_block(step):
         lanes = slice(step * cap, (step + 1) * cap)
         rows_t = cmall[56:57, lanes].astype(jnp.int32)
-        cols_t = cmall[57:58, lanes].astype(jnp.int32) + 5
+        cols_t = cmall[57:58, lanes].astype(jnp.int32) - 3
         placed = []
         for r in range(rows_n):
             value = jnp.zeros((8, cap), F32)
@@ -179,20 +199,41 @@
                     value = jnp.where(rows_t == r - i, cmall[8 * i : 8 * i + 8, lanes], value)
             placed.append(value)
 
-        @pl.loop(0, WIDE // 16)
-        def _(tile):
-            offset = lax.broadcasted_iota(jnp.int32, (16, cap), 0) + tile * 16 - cols_t
+        def tiles(column, base, stride):
+            offset = column - cols_t
             hits = [offset == j for j in range(WIN)]
             for r in range(rows_n):
                 value = jnp.zeros((16, cap), F32)
                 for j in range(WIN):
                     value = jnp.where(hits[j], placed[r][j : j + 1, :], value)
-                start = pl.multiple_of(r * WIDE + tile * 16, 16)
+                start = pl.multiple_of(r * stride + base, 16)
                 spread[pl.ds(start, 16), lanes] = value.astype(BF)
 
-    fill(hext, h_ref)
-    fill(xext, x_ref)
+        count = lax.broadcasted_iota(jnp.int32, (16, cap), 0)
+
+        @pl.loop(0, cols_n // 16)
+        def _(tile):
+            tiles(count + tile * 16, tile * 16, cols_n)
+
+        tiles(jnp.where(count < 8, count - 8, count + (cols_n - 8)), cells, EDGE)
+
+    hext[...] = jnp.zeros_like(hext)
     gext[...] = jnp.zeros_like(gext)
+    pext[...] = jnp.zeros_like(pext)
+
+    @pl.loop(0, rows_n)
+    def _(r):
+        hext[r + 1, 16 : 16 + cols_n, :] = h_ref[r].astype(F32)
+
+    for wide in (xh, xg, xp):
+        wide[0:cols_n, :] = jnp.zeros((cols_n, 3 * chans), BF)
+        wide[cells + cols_n :, :] = jnp.zeros((cols_n, 3 * chans), BF)
+    for thin in (xhm, xgm, xpm):
+        thin[0:EDGE, :] = jnp.zeros((EDGE, 3 * chans), BF)
+        thin[rim + EDGE :, :] = jnp.zeros((EDGE, 3 * chans), BF)
+
+    turned(h_ref, ht)
+    turned(x_ref, xt)
     spread_block(0)
 
     for step in range(1, lon_n):
@@ -201,25 +242,33 @@
         cmall[:, step * cap : (step + 1) * cap] = pay_recv[step - 1, cap : cap + 64, :].astype(F32)
         spread_block(step)
 
-    for side in range(2):
-        halos[side].wait()
+    def to_rim(ext, block):
+        block = block.reshape(rows_n, EDGE, chans)
+        ext[1 : 1 + rows_n, 8:16, :] = block[:, 0:8]
+        ext[1 : 1 + rows_n, 16 + cols_n : 24 + cols_n, :] = block[:, 8:16]
+
+    for g in range(rows_n // BAND):
+        low = g * BAND * cols_n
+        block = dot(spread[pl.ds(low, BAND * cols_n), :], qall[...])
+        gext[pl.ds(1 + g * BAND, BAND), 16 : 16 + cols_n, :] = block.reshape(BAND, cols_n, chans)
+
+    to_rim(gext, dot(spread[cells : cells + rim, :], qall[...]))
+    for copy in halos:
+        copy.wait()
+
+    def unpack(side, first, count, out_at, in_edge):
         strip[...] = halo_recv[side].astype(F32)
         for r in range(rows_n):
-            h_edge = strip[HALO * r : HALO * r + 4, :]
-            x_edge = strip[HALO * r + 4 : HALO * r + 9, :]
-            if side == 0:
-                hext[r + 1, 12:16, :] = h_edge
-                xext[r + 1, 11:16, :] = x_edge
-            else:
-                hext[r + 1, 16 + cols_n : 20 + cols_n, :] = h_edge
-                xext[r + 1, 16 + cols_n : 21 + cols_n, :] = x_edge
-    side_by_side(hext, xh)
-
-    for g in range(2):
-        cells = slice(g * half * WIDE, (g + 1) * half * WIDE)
-        block = dot(spread[cells, :], qall[...])
-        gext[1 + g * half : 1 + (g + 1) * half, 8 : 8 + WIDE, :] = block.reshape(half, WIDE, chans)
-        gt[:, g * half * WIDE : (g + 1) * half * WIDE] = block.T.astype(BF)
+            at = HALO * r + first
+            edge[r + 1, in_edge : in_edge + count, :] = strip[at : at + count, :]
+            if out_at:
+                hext[r + 1, out_at : out_at + count, :] = strip[at : at + count, :]
+
+    edge[...] = jnp.zeros_like(edge)
+    unpack(0, 0, 4, 12, 4)
+    unpack(1, 0, 4, 16 + cols_n, 8)
+    turned_edge(ht)
+    side_by_side(gext, xg, xgm, True)
 
     def halves(which):
         return remote(
@@ -246,13 +295,16 @@
             ag.at[which], outs[which].at[core], pair_s.at[which], pair_r.at[which], pair
         )
 
-    def weight_terms(which, source):
+    def weight_terms(which, turned_source, grad, grad_edge):
+        term = dot(turned_source[:, 0:cells], grad[cols_n : cols_n + cells, :])
+        term = term + dot(turned_source[:, cells : cells + rim], grad_edge[EDGE : EDGE + rim, :])
+        term = term * scale
         for a in range(3):
-            block = source[a : a + rows_n].reshape(rows_n * WIDE, 3 * chans)
-            term = dot(gt[...], block) * scale
             for b in range(3):
                 row = (3 * a + b) * chans
-                grads[which, row : row + chans, :] = term[:, b * chans : (b + 1) * chans].T
+                grads[which, row : row + chans, :] = term[
+                    a * chans : (a + 1) * chans, b * chans : (b + 1) * chans
+                ]
         other = pl.ds(pl.multiple_of((1 - core) * part, 8), part)
         half_send[which] = grads[which, other, :].astype(BF)
         halves(which).start()
@@ -287,13 +339,23 @@
         pairs(which).start()
         outs[which][core] = ag[which]
 
-    weight_terms(0, xh)
-
-    for g in range(2):
-        feat[g * half * WIDE : (g + 1) * half * WIDE, :] = conv(xh, w_ref, g * half).astype(BF)
-    slot_grads = lax.dot_general(
-        feat[...], spread[...], (((0,), (0,)), ((), ())), preferred_element_type=F32
-    )
+    weight_terms(0, ht, xg, xgm)
+
+    edge[...] = jnp.zeros_like(edge)
+    unpack(0, 4, 5, 0, 3)
+    unpack(1, 4, 5, 0, 8)
+    turned_edge(xt)
+
+    side_by_side(hext, xh, xhm, False)
+    for g in range(rows_n // BAND):
+        low = g * BAND * cols_n
+        block = conv(xh, w_ref, low, BAND * cols_n, cols_n)
+        feat_t[:, pl.ds(low, BAND * cols_n)] = block.T.astype(BF)
+
+    feat_t[:, cells : cells + rim] = conv(xhm, w_ref, 0, rim, EDGE).T.astype(BF)
+
+    scatter_start(0)
+    slot_grads = dot(feat_t[...], spread[...])
     retall[:, 0:cap] = slot_grads[:, 0:cap].astype(BF)
     returns = []
     for step in range(1, lon_n):
@@ -305,17 +367,24 @@
         copy.start()
         returns.append(copy)
 
-    scatter_start(0)
-    side_by_side(gext, xg)
-    side_by_side(xext, xx)
-    for g in range(2):
-        back = conv(xg, wb, g * half).reshape(half, WIDE, chans)
-        active = hext[1 + g * half : 1 + (g + 1) * half, 8 : 8 + WIDE, :] > 0
-        block = jnp.where(active, back, 0.0).reshape(half * WIDE, chans)
-        gt[:, g * half * WIDE : (g + 1) * half * WIDE] = block.T.astype(BF)
-    weight_terms(1, xx)
+    for g in range(rows_n // BAND):
+        low = g * BAND * cols_n
+        back = conv(xg, wb, low, BAND * cols_n, cols_n).reshape(BAND, cols_n, chans)
+        rows = pl.ds(1 + g * BAND, BAND)
+        active = hext[rows, 16 : 16 + cols_n, :] > 0
+        pext[rows, 16 : 16 + cols_n, :] = jnp.where(active, back, 0.0)
+
+    rim_active = jnp.concatenate(
+        [hext[1 : 1 + rows_n, 8:16, :], hext[1 : 1 + rows_n, 16 + cols_n : 24 + cols_n, :]],
+        axis=1,
+    ).reshape(rim, chans) > 0
+    to_rim(pext, jnp.where(rim_active, conv(xgm, wb, 0, rim, EDGE), 0.0))
+    side_by_side(pext, xp, xpm, True)
+    weight_terms(1, xt, xp, xpm)
 
     scatter_start(1)
+    gather_start(0)
+    gather_start(1)
     for step in range(1, lon_n):
         returns[step - 1].wait()
         retall[:, step * cap : (step + 1) * cap] = ret_recv[step - 1]
@@ -334,15 +403,13 @@
         copy.start()
         qgs.append(copy)
 
-    gather_start(0)
-    gather_start(1)
     pair_start(0)
+    pair_start(1)
     total = qg_own[frame]
     for step in range(1, frame_n):
         qgs[step - 1].wait()
         total = total + qg_recv[step - 1].astype(F32)
     query_out[...] = total
-    pair_start(1)
     pairs(0).wait()
     pairs(1).wait()
 
@@ -380,13 +447,18 @@
         vm((rows_n + 2, EXT, chans), F32),
         vm((rows_n + 2, EXT, chans), F32),
         vm((rows_n + 2, EXT, chans), F32),
-        vm((rows_n + 2, WIDE, 3 * chans), BF),
-        vm((rows_n + 2, WIDE, 3 * chans), BF),
-        vm((rows_n + 2, WIDE, 3 * chans), BF),
-        vm((rows_n * WIDE, chans), BF),
+        vm(((rows_n + 2) * cols_n, 3 * chans), BF),
+        vm(((rows_n + 2) * EDGE, 3 * chans), BF),
+        vm(((rows_n + 2) * cols_n, 3 * chans), BF),
+        vm(((rows_n + 2) * EDGE, 3 * chans), BF),
+        vm(((rows_n + 2) * cols_n, 3 * chans), BF),
+        vm(((rows_n + 2) * EDGE, 3 * chans), BF),
+        vm((chans, rows_n * (cols_n + EDGE)), BF),
         vm((3, 3 * chans, chans), BF),
-        vm((chans, rows_n * WIDE), BF),
-        vm((rows_n * WIDE, slots), BF),
+        vm((3 * chans, rows_n * (cols_n + EDGE)), BF),
+        vm((3 * chans, rows_n * (cols_n + EDGE)), BF),
+        vm((rows_n * (cols_n + EDGE), slots), BF),
+        vm((rows_n + 2, EDGE, chans), F32),
         vm((64, tracks), F32),
         vm((slots, tracks), BF),
         vm((slots, chans), BF),

time: 42.3 us -> 40.6 us (0.960)
  Pallas kernels: 41.5 us -> 39.8 us
    pallas_call x1, Pallas kernels: 39.3 us -> 37.7 us  [per_device(): pl.pallas_call(functools.partial(kernel, dims), out_shape=(jax.ShapeDtype...]
where the time goes in v2:
time: 40.6 us; the launch traced here: 40.5 us
  Pallas kernels  39.8 us (98%)
  between operations  0.64 us (2%)
    pallas_call x1, Pallas kernels, per_device(): pl.pallas_call(functools.partial(kernel, dims), out_shape=(jax.ShapeDtype...  37.7 us
    pallas_call x1, Pallas kernels, per_device(): pl.pallas_call(functools.partial(expand, (part, group_n, chunk)), out_sha...  2.14 us

profile of v2, /device:TPU:0, one launch (start us, length us, event | category | flops | bytes accessed | tf_op | source)
XLA Modules:
  0.0 40.5 jit_solution(9578978834531823909)
XLA Ops:
  0.6 37.7 %shard_map.103 = (f32[64,128]{1,0:T(8,128)}, bf16[2,16,36,128]{3,2,1,0:T(8,128)(2,1)}, bf16[2,16,36,128]{3,2,1,0:T(8,128)(2,1)}) custom-call(bf16[16,128,128]{2,1,0:T(8,128)(2,1)} %bitcast.7, bf16[16,128,128]{2,1,0:T(8,128)(2,1)} %bitcast.8, bf16[3,384,128]{2,1,0:T(8,128)(2,1)} %bitcast.9, bf16[512,128]{1,0:T(8,128)(2,1)} %q_ref.1, ...), custom_call_target="tpu_custom_call" | custom-call | tf_op jit(solution)/shard_map/pallas_call | solution.py:495
  38.3 2.1 %shard_map.104 = (f32[64,128]{1,0:T(8,128)}, f32[1152,128]{1,0:T(8,128)}, f32[1152,128]{1,0:T(8,128)}) custom-call(f32[64,128]{1,0:T(8,128)} %get-tuple-element.9.query_ref, bf16[2,16,36,128]{3,2,1,0:T(8,128)(2,1)} %get-tuple-element.10.first_ref, bf16[2,16,36,128]{3,2,1,0:T(8,128)(2,1)} %get-tuple-element.11.second_ref), custom_call_target="tpu_custom_call" | custom-call | tf_op jit(solution)/shard_map/pallas_call | solution.py:509

commit v3 on v2

--- a/solution.py
+++ b/solution.py
@@ -346,7 +346,24 @@
     unpack(1, 4, 5, 0, 8)
     turned_edge(xt)
 
+    for g in range(rows_n // BAND):
+        low = g * BAND * cols_n
+        back = conv(xg, wb, low, BAND * cols_n, cols_n).reshape(BAND, cols_n, chans)
+        rows = pl.ds(1 + g * BAND, BAND)
+        active = hext[rows, 16 : 16 + cols_n, :] > 0
+        pext[rows, 16 : 16 + cols_n, :] = jnp.where(active, back, 0.0)
+
+    rim_active = jnp.concatenate(
+        [hext[1 : 1 + rows_n, 8:16, :], hext[1 : 1 + rows_n, 16 + cols_n : 24 + cols_n, :]],
+        axis=1,
+    ).reshape(rim, chans) > 0
+    to_rim(pext, jnp.where(rim_active, conv(xgm, wb, 0, rim, EDGE), 0.0))
+    scatter_start(0)
+    side_by_side(pext, xp, xpm, True)
+    weight_terms(1, xt, xp, xpm)
+
     side_by_side(hext, xh, xhm, False)
+    scatter_start(1)
     for g in range(rows_n // BAND):
         low = g * BAND * cols_n
         block = conv(xh, w_ref, low, BAND * cols_n, cols_n)
@@ -354,7 +371,6 @@
 
     feat_t[:, cells : cells + rim] = conv(xhm, w_ref, 0, rim, EDGE).T.astype(BF)
 
-    scatter_start(0)
     slot_grads = dot(feat_t[...], spread[...])
     retall[:, 0:cap] = slot_grads[:, 0:cap].astype(BF)
     returns = []
@@ -367,22 +383,6 @@
         copy.start()
         returns.append(copy)
 
-    for g in range(rows_n // BAND):
-        low = g * BAND * cols_n
-        back = conv(xg, wb, low, BAND * cols_n, cols_n).reshape(BAND, cols_n, chans)
-        rows = pl.ds(1 + g * BAND, BAND)
-        active = hext[rows, 16 : 16 + cols_n, :] > 0
-        pext[rows, 16 : 16 + cols_n, :] = jnp.where(active, back, 0.0)
-
-    rim_active = jnp.concatenate(
-        [hext[1 : 1 + rows_n, 8:16, :], hext[1 : 1 + rows_n, 16 + cols_n : 24 + cols_n, :]],
-        axis=1,
-    ).reshape(rim, chans) > 0
-    to_rim(pext, jnp.where(rim_active, conv(xgm, wb, 0, rim, EDGE), 0.0))
-    side_by_side(pext, xp, xpm, True)
-    weight_terms(1, xt, xp, xpm)
-
-    scatter_start(1)
     gather_start(0)
     gather_start(1)
     for step in range(1, lon_n):

time: 40.6 us -> 38.9 us (0.958)
  Pallas kernels: 39.8 us -> 38.1 us
    pallas_call x1, Pallas kernels: 37.7 us -> 36 us  [per_device(): pl.pallas_call(functools.partial(kernel, dims), out_shape=(jax.ShapeDtype...]
where the time goes in v3:
time: 38.9 us; the launch traced here: 38.8 us
  Pallas kernels  38.1 us (98%)
  between operations  0.64 us (2%)
    pallas_call x1, Pallas kernels, per_device(): pl.pallas_call(functools.partial(kernel, dims), out_shape=(jax.ShapeDtype...  36 us
    pallas_call x1, Pallas kernels, per_device(): pl.pallas_call(functools.partial(expand, (part, group_n, chunk)), out_sha...  2.14 us

profile of v3, /device:TPU:0, one launch (start us, length us, event | category | flops | bytes accessed | tf_op | source)
XLA Modules:
  0.0 38.8 jit_solution(6653621752130164531)
XLA Ops:
  0.6 36.0 %shard_map.103 = (f32[64,128]{1,0:T(8,128)}, bf16[2,16,36,128]{3,2,1,0:T(8,128)(2,1)}, bf16[2,16,36,128]{3,2,1,0:T(8,128)(2,1)}) custom-call(bf16[16,128,128]{2,1,0:T(8,128)(2,1)} %bitcast.7, bf16[16,128,128]{2,1,0:T(8,128)(2,1)} %bitcast.8, bf16[3,384,128]{2,1,0:T(8,128)(2,1)} %bitcast.9, bf16[512,128]{1,0:T(8,128)(2,1)} %q_ref.1, ...), custom_call_target="tpu_custom_call" | custom-call | tf_op jit(solution)/shard_map/pallas_call | solution.py:495
  36.6 2.1 %shard_map.104 = (f32[64,128]{1,0:T(8,128)}, f32[1152,128]{1,0:T(8,128)}, f32[1152,128]{1,0:T(8,128)}) custom-call(f32[64,128]{1,0:T(8,128)} %get-tuple-element.9.query_ref, bf16[2,16,36,128]{3,2,1,0:T(8,128)(2,1)} %get-tuple-element.10.first_ref, bf16[2,16,36,128]{3,2,1,0:T(8,128)(2,1)} %get-tuple-element.11.second_ref), custom_call_target="tpu_custom_call" | custom-call | tf_op jit(solution)/shard_map/pallas_call | solution.py:509

commit v4 on v3

--- a/solution.py
+++ b/solution.py
@@ -58,7 +58,8 @@
         return lax.rem(frame + steps + frame_n, frame_n)
 
     def group_id(steps):
-        return lax.rem(place + steps, group_n)
+        chip = lax.rem(lon // 2 + steps % (lon_n // 2), lon_n // 2)
+        return chip * frame_n + lax.rem(frame + steps // (lon_n // 2), frame_n)
 
     def group_device(p):
         return {"lon": (p // frame_n) * 2 + core, "frame": lax.rem(p, frame_n)}

time: 38.9 us -> 38.7 us (level)
  no operation moved by 1% of the time
where the time goes in v4:
time: 38.7 us; the launch traced here: 38.6 us
  Pallas kernels  37.9 us (98%)
  between operations  0.64 us (2%)
    pallas_call x1, Pallas kernels, per_device(): pl.pallas_call(functools.partial(kernel, dims), out_shape=(jax.ShapeDtype...  35.8 us
    pallas_call x1, Pallas kernels, per_device(): pl.pallas_call(functools.partial(expand, (part, group_n, chunk)), out_sha...  2.14 us

profile of v4, /device:TPU:0, one launch (start us, length us, event | category | flops | bytes accessed | tf_op | source)
XLA Modules:
  0.0 38.6 jit_solution(15557046104579094392)
XLA Ops:
  0.6 35.8 %shard_map.103 = (f32[64,128]{1,0:T(8,128)}, bf16[2,16,36,128]{3,2,1,0:T(8,128)(2,1)}, bf16[2,16,36,128]{3,2,1,0:T(8,128)(2,1)}) custom-call(bf16[16,128,128]{2,1,0:T(8,128)(2,1)} %bitcast.7, bf16[16,128,128]{2,1,0:T(8,128)(2,1)} %bitcast.8, bf16[3,384,128]{2,1,0:T(8,128)(2,1)} %bitcast.9, bf16[512,128]{1,0:T(8,128)(2,1)} %q_ref.1, ...), custom_call_target="tpu_custom_call" | custom-call | tf_op jit(solution)/shard_map/pallas_call | solution.py:496
  36.4 2.1 %shard_map.104 = (f32[64,128]{1,0:T(8,128)}, f32[1152,128]{1,0:T(8,128)}, f32[1152,128]{1,0:T(8,128)}) custom-call(f32[64,128]{1,0:T(8,128)} %get-tuple-element.9.query_ref, bf16[2,16,36,128]{3,2,1,0:T(8,128)(2,1)} %get-tuple-element.10.first_ref, bf16[2,16,36,128]{3,2,1,0:T(8,128)(2,1)} %get-tuple-element.11.second_ref), custom_call_target="tpu_custom_call" | custom-call | tf_op jit(solution)/shard_map/pallas_call | solution.py:510
